TPU v7x, 32 devices: a whole 2x2x4 slice. The times are simulated.
32 devices in a mesh: group: 2 (over y), tile: 4 (over z), dp: 2 (over x), chan: 2 (over core).
Axes of the slice: x: 2, y: 2, z: 4, core: 2. Of those that a mesh axis runs over, the one named last changes fastest.
Arguments:
- inputs: bfloat16 [4, 4, 32, 32, 128], P(('group', 'dp'), 'tile'), parts along dimension 0, may hold values from -6 to 6
- kernel: float32 [49, 128], replicated, may hold values from -0.875 to 0.875
- norm_gain: float32 [128], replicated, may hold values from 0.1 to 1.9
- w_in: bfloat16 [128, 512], P(None, 'chan'), may hold values from -0.5 to 0.5
- w_out: bfloat16 [512, 128], P('chan'), may hold values from -0.25 to 0.25
- layer_scale: float32 [128], replicated, may hold values from 0.25 to 2
- cotangent: bfloat16 [4, 4, 32, 32, 128], P(('group', 'dp'), 'tile'), parts along dimension 0, may hold values from -6 to 6
- adjacency: int32 [4, 8, 2], replicated, may hold values from 0 to 3
Outputs:
- inputs_grad: bfloat16 [4, 4, 32, 32, 128], P(('group', 'dp'), 'tile'), parts along dimension 0
- kernel_grad: float32 [98, 128], P('group'), parts along dimension 0
- gain_grad: float32 [256], P('group'), parts along dimension 0
- w_in_grad: float32 [256, 512], P(('group', 'dp'), 'chan'), parts along dimension 0
- w_out_grad: float32 [1024, 128], P(('group', 'chan'), 'dp'), parts along dimension 0
- scale_grad: float32 [256], P('group'), parts along dimension 0
There are 2 independent parts, one for each index of `group`. A program takes and returns all parts, laid end to end along the dimension named above; an argument that names none is the same for every part. Nothing has to cross between parts.
Inputs may be any that keep to these rules, and one draw needn't show every extreme that they name: The tiles form a closed band of two rows of 2 tiles, a stand-in for a sphere's tiling with rotated neighbours, with consistent neighbours; every tile is some tile's neighbour.
All inputs are finite; a program needn't handle non-finite values.
Results may differ from a plain program's by a relative error of at most 0.0063.
Values may be sent and summed in bfloat16 or wider, within the bound.
A program may use at most 64 MiB of HBM per device.

v0:
```python
import math

import jax
import jax.numpy as jnp
from jax import lax
from jax.sharding import PartitionSpec as P

KS = 7


eps = 1e-06
root_two_pi = 0.7978845608028654
cubic_coef = 0.044715
facing_turns = (2, 3, 0, 1, 2, 0, 0, 2)
corner_at_end = (True, False, True, False)


def gelu_pair(values):
    inner = root_two_pi * (values + cubic_coef * values * values * values)
    tanh_part = jnp.tanh(inner)
    active = 0.5 * values * (1.0 + tanh_part)
    gelu_slope = 0.5 * (1.0 + tanh_part) + 0.5 * values * (
        1.0 - tanh_part * tanh_part
    ) * root_two_pi * (1.0 + 3.0 * cubic_coef * values * values)
    return (active, gelu_slope)


def norm_forward(conv_flat, norm_gain):
    row_mean = jnp.mean(conv_flat, axis=1, keepdims=True)
    centred = conv_flat - row_mean
    inv_std = lax.rsqrt(jnp.mean(centred * centred, axis=1, keepdims=True) + eps)
    normed = centred * inv_std
    return (normed, inv_std, (normed * norm_gain).astype(jnp.bfloat16))


def norm_backward(normed_grad, normed, inv_std, norm_gain):
    scaled = normed_grad * norm_gain
    first_mean = jnp.mean(scaled, axis=1, keepdims=True)
    second_mean = jnp.mean(scaled * normed, axis=1, keepdims=True)
    return (inv_std * (scaled - first_mean - normed * second_mean)).astype(jnp.bfloat16)


def pointwise(conv_flat, upstream_flat, norm_gain, w_in, w_out, layer_scale, combine_rows):
    normed, inv_std, normed_b = norm_forward(conv_flat, norm_gain)
    hidden = jnp.dot(normed_b, w_in, preferred_element_type=jnp.float32)
    active, gelu_slope = gelu_pair(hidden)
    active_b = active.astype(jnp.bfloat16)
    branch = jnp.dot(active_b, w_out, preferred_element_type=jnp.float32)
    scale_part = jnp.sum(upstream_flat * branch, axis=0)
    scaled_b = (upstream_flat * layer_scale).astype(jnp.bfloat16)
    w_out_part = jnp.dot(active_b.T, scaled_b, preferred_element_type=jnp.float32)
    hidden_grad = (
        jnp.dot(scaled_b, w_out.T, preferred_element_type=jnp.float32) * gelu_slope
    ).astype(jnp.bfloat16)
    w_in_part = jnp.dot(normed_b.T, hidden_grad, preferred_element_type=jnp.float32)
    normed_part = jnp.dot(hidden_grad, w_in.T, preferred_element_type=jnp.float32)
    gain_part = jnp.sum(normed_part * normed, axis=0)
    normed_grad = combine_rows(normed_part)
    conv_grad = norm_backward(normed_grad, normed, inv_std, norm_gain)
    return (conv_grad, w_in_part, w_out_part, gain_part, scale_part)


def depthwise(padded, kernel, row_count):
    rim_width = KS // 2
    rows = lax.slice_in_dim(padded, 0, row_count + 2 * rim_width, axis=1)
    tile_side = padded.shape[2] - 2 * rim_width
    summed = jnp.zeros((rows.shape[0], row_count, tile_side, rows.shape[3]), jnp.float32)
    for shift_row in range(KS):
        for shift_col in range(KS):
            summed = (
                summed
                + rows[
                    :, shift_row : shift_row + row_count, shift_col : shift_col + tile_side
                ].astype(jnp.float32)
                * kernel[shift_row * KS + shift_col]
            )
    return summed


def kernel_terms(rows, conv_grad):
    row_count, tile_side = (conv_grad.shape[1], conv_grad.shape[2])
    grad_f = conv_grad.astype(jnp.float32)
    terms = []
    for shift_row in range(KS):
        for shift_col in range(KS):
            window = rows[
                :, shift_row : shift_row + row_count, shift_col : shift_col + tile_side
            ].astype(jnp.float32)
            terms.append(jnp.sum(window * grad_f, axis=(0, 1, 2)))
    return jnp.stack(terms, axis=0)


def spread_back(conv_grad, kernel):
    edge = 2 * (KS // 2)
    tile_side = conv_grad.shape[1]
    grad_pad = jnp.pad(conv_grad.astype(jnp.float32), ((0, 0), (edge, edge), (edge, edge), (0, 0)))
    summed = jnp.zeros(
        (conv_grad.shape[0], tile_side + edge, tile_side + edge, conv_grad.shape[3]), jnp.float32
    )
    for shift_row in range(KS):
        for shift_col in range(KS):
            window = grad_pad[
                :,
                edge - shift_row : edge - shift_row + tile_side + edge,
                edge - shift_col : edge - shift_col + tile_side + edge,
            ]
            summed = summed + kernel[shift_row * KS + shift_col] * window
    return summed


def corner_cut(strip, slot_index, rim_width):
    if slot_index in (4, 6):
        return strip[..., -rim_width:, :]
    return strip[..., :rim_width, :]


def corner_strip(corner, corner_slot, tile_side, rim_width):
    filler = jnp.zeros(corner.shape[:2] + (tile_side - rim_width, corner.shape[3]), jnp.float32)
    if corner_at_end[corner_slot]:
        return jnp.concatenate([filler, corner], axis=2)
    return jnp.concatenate([corner, filler], axis=2)


def on_device(inputs, kernel, norm_gain, w_in, w_out, layer_scale, cotangent, adjacency):
    rim_width = KS // 2
    samples, tile_side, channels = (inputs.shape[0], inputs.shape[2], inputs.shape[4])
    tile_count = lax.axis_size("tile")
    own_tile = lax.axis_index("tile")
    centre = inputs[:, 0]
    upstream = cotangent[:, 0]
    faces_out = jnp.stack(
        [
            centre[:, :rim_width],
            jnp.rot90(centre[:, :, -rim_width:], 1, axes=(1, 2)),
            jnp.rot90(centre[:, -rim_width:], 2, axes=(1, 2)),
            jnp.rot90(centre[:, :, :rim_width], 3, axes=(1, 2)),
        ],
        axis=0,
    )
    strip_zero = jnp.zeros((samples, rim_width, tile_side, channels), jnp.bfloat16)
    partial_value = tuple((strip_zero for slot_index in range(8)))
    shards = lax.all_gather(faces_out[None], "tile", axis=0, tiled=True)
    shard_count = shards.shape[0]
    chosen_list = []
    for take_slot_index in range(8):
        source = adjacency[own_tile, take_slot_index, 0]
        face_index = (adjacency[own_tile, take_slot_index, 1] + facing_turns[take_slot_index]) % 4
        inside = (source >= 0) & (source < shard_count)
        chosen = lax.dynamic_index_in_dim(
            shards, jnp.clip(source, 0, shard_count - 1), 0, keepdims=False
        )
        chosen = lax.dynamic_index_in_dim(chosen, face_index, 0, keepdims=False)
        chosen_list.append(jnp.where(inside, chosen, partial_value[take_slot_index]))
    canon = tuple(chosen_list)
    edge_canon = [canon[slot_index] for slot_index in range(4)]
    corner_canon = [
        corner_cut(canon[slot_index], slot_index, rim_width) for slot_index in range(4, 8)
    ]
    north = jnp.rot90(edge_canon[0], 2, axes=(1, 2))
    east = jnp.rot90(edge_canon[1], 1, axes=(1, 2))
    south = edge_canon[2]
    west = jnp.rot90(edge_canon[3], -1, axes=(1, 2))
    north_east = jnp.rot90(corner_canon[0], 2, axes=(1, 2))
    south_east = corner_canon[1]
    south_west = corner_canon[2]
    north_west = jnp.rot90(corner_canon[3], 2, axes=(1, 2))
    top_rows = jnp.concatenate([north_west, north, north_east], axis=2)
    middle_rows = jnp.concatenate([west, centre, east], axis=2)
    bottom_rows = jnp.concatenate([south_west, south, south_east], axis=2)
    padded = jnp.concatenate([top_rows, middle_rows, bottom_rows], axis=1)
    half_rows = tile_side // lax.axis_size("chan")
    first_row = lax.axis_index("chan") * half_rows
    conv = depthwise(padded, kernel, tile_side)
    conv_grad, w_in_part, w_out_part, gain_part, scale_part = pointwise(
        conv.reshape(-1, channels),
        upstream.reshape(-1, channels).astype(jnp.float32),
        norm_gain,
        w_in,
        w_out,
        layer_scale,
        lambda rows_part: lax.psum(rows_part, "chan"),
    )
    conv_grad = conv_grad.reshape(samples, tile_side, tile_side, channels)
    own_grad = lax.dynamic_slice_in_dim(conv_grad, first_row, half_rows, 1)
    own_rows = lax.dynamic_slice_in_dim(padded, first_row, half_rows + 2 * rim_width, 1)
    kernel_part = kernel_terms(own_rows, own_grad)
    pad_grad = spread_back(conv_grad, kernel)
    edge_slots = jnp.stack(
        [
            jnp.rot90(pad_grad[:, :rim_width, rim_width:-rim_width], 2, axes=(1, 2)),
            jnp.rot90(pad_grad[:, rim_width:-rim_width, -rim_width:], -1, axes=(1, 2)),
            pad_grad[:, -rim_width:, rim_width:-rim_width],
            jnp.rot90(pad_grad[:, rim_width:-rim_width, :rim_width], 1, axes=(1, 2)),
        ],
        axis=0,
    )
    corner_slots = jnp.stack(
        [
            jnp.rot90(pad_grad[:, :rim_width, -rim_width:], 2, axes=(1, 2)),
            pad_grad[:, -rim_width:, -rim_width:],
            pad_grad[:, -rim_width:, :rim_width],
            jnp.rot90(pad_grad[:, :rim_width, :rim_width], 2, axes=(1, 2)),
        ],
        axis=0,
    )
    sides_zero = jnp.zeros((4, samples, rim_width, tile_side, channels), jnp.float32)
    collected = sides_zero
    edge_shards = lax.all_gather(edge_slots[None], "tile", axis=0, tiled=True)
    corner_shards = lax.all_gather(corner_slots[None], "tile", axis=0, tiled=True)

    def per_tile(position, collected):
        edge_grads = lax.dynamic_index_in_dim(edge_shards, position, 0, keepdims=False)
        corner_grads = lax.dynamic_index_in_dim(corner_shards, position, 0, keepdims=False)
        for slot_index in range(8):
            matches = adjacency[position, slot_index, 0] == own_tile
            face_index = (adjacency[position, slot_index, 1] + facing_turns[slot_index]) % 4
            if slot_index < 4:
                piece = edge_grads[slot_index]
            else:
                piece = corner_strip(
                    corner_grads[slot_index - 4], slot_index - 4, tile_side, rim_width
                )
            current = lax.dynamic_index_in_dim(collected, face_index, 0, keepdims=False)
            updated = current + jnp.where(matches, piece, 0.0)
            collected = lax.dynamic_update_index_in_dim(collected, updated, face_index, 0)
        return collected

    incoming = lax.fori_loop(0, edge_shards.shape[0], per_tile, collected)
    summed = upstream.astype(jnp.float32) + pad_grad[:, rim_width:-rim_width, rim_width:-rim_width]
    summed = summed.at[:, :rim_width, :].add(incoming[0])
    summed = summed.at[:, :, -rim_width:].add(jnp.rot90(incoming[1], -1, axes=(1, 2)))
    summed = summed.at[:, -rim_width:, :].add(jnp.rot90(incoming[2], 2, axes=(1, 2)))
    summed = summed.at[:, :, :rim_width].add(jnp.rot90(incoming[3], 1, axes=(1, 2)))
    factor = 1.0 / math.sqrt(samples * lax.axis_size("dp") * tile_count * tile_side * tile_side)
    kernel_sum, gain_sum, scale_sum = lax.psum(
        (kernel_part, gain_part, scale_part), ("tile", "dp", "chan")
    )
    w_in_tile, w_out_tile = lax.psum((w_in_part, w_out_part), "tile")
    w_in_sum, w_out_sum = (
        lax.psum_scatter(w_in_tile, "dp", scatter_dimension=0, tiled=True),
        lax.psum_scatter(w_out_tile, "dp", scatter_dimension=1, tiled=True),
    )
    return (
        summed[:, None].astype(jnp.bfloat16),
        kernel_sum * factor,
        gain_sum * factor,
        w_in_sum * factor,
        w_out_sum * factor,
        scale_sum * factor,
    )


def solution(mesh):
    placed = (
        P(("group", "dp"), "tile", None, None, None),
        P(),
        P(),
        P(None, "chan"),
        P("chan", None),
        P(),
        P(("group", "dp"), "tile", None, None, None),
        P(),
    )
    return jax.shard_map(
        on_device,
        mesh=mesh,
        in_specs=placed,
        out_specs=(
            P(("group", "dp"), "tile", None, None, None),
            P("group", None),
            P("group"),
            P(("group", "dp"), "chan"),
            P(("group", "chan"), "dp"),
            P("group"),
        ),
        check_vma=False,
    )
```

profile of v0, /device:TPU:0, one launch (start us, length us, event | category | flops | bytes accessed | tf_op | source)
XLA Modules:
  0.0 316.1 jit_solution(2402869062915067716)
XLA Ops:
  7.2 2.0 constant_dynamic-slice_fusion.40
  33.3 0.9 slice_bitcast_fusion.56
  34.3 1.0 slice_bitcast_fusion.58
  35.3 1.0 slice_bitcast_fusion.57
  36.3 1.1 copy.106
  37.7 16.2 %all-gather = bf16[16,1,3,32,128]{4,3,2,1,0:T(8,128)(2,1)S(1)} all-gather(bf16[4,1,3,32,128]{4,3,2,1,0:T(8,128)(2,1)S(1)} %pad_maximum_fusion.3), channel_id=2, replica_groups=mesh['group'=2,'tile'=4,'dp'=2,'chan'=2] {'tile'}, dimensions={0}, use_global_device_ids=true | all-gather | bytes 491520 | tf_op jit(solution)/shard_map/all_gather | solution.py:142
  54.9 4.7 %fusion.134 = (f32[32,32]{0,1:T(8,128)S(1)}, f32[1,32,32,128]{3,1,2,0:T(8,128)S(1)}) fusion(f32[128]{0:T(128)S(1)} %get-tuple-element.418, bf16[1,35,38,128]{3,1,2,0:T(8,128)(2,1)S(1)} %get-tuple-element.364, f32[128]{0:T(128)S(1)} %get-tuple-element.419, f32[128]{0:T(128)S(1)} %get-tuple-element.372, f32[128]{0:T(128)S(1)} %get-tuple-element.373, ...), kind=kLoop, calls=%fused_computation.413 | loop fusion | flops 20052992 | bytes 11874816 | tf_op jit(solution)/shard_map/reduce_sum | solution.py:29
  62.5 0.8 fusion.12
  63.3 0.9 fusion.139
  64.3 0.9 fusion.140
  65.3 11.1 %reduce-scatter.3.cloned.1.call-done = f32[64,256]{1,0:T(8,128)} async-done(((f32[128,256]{1,0:T(8,128)}), f32[64,256]{1,0:T(8,128)}) %reduce-scatter.3.cloned.1.call-update) | async-done | bytes 65552 | tf_op jit(solution)/shard_map/reduce_scatter | solution.py:240
  76.4 12.5 %reduce-scatter.5.cloned.1.call-done = f32[256,64]{0,1:T(8,128)} async-done(((f32[256,128]{0,1:T(8,128)}), f32[256,64]{0,1:T(8,128)}) %reduce-scatter.5.cloned.1.call-update) | async-done | bytes 65552 | tf_op jit(solution)/shard_map/reduce_scatter | solution.py:241
  89.1 1.1 fusion.138
  90.7 0.7 fusion.125
  91.4 34.4 %all-reduce.12.cloned.1.call-done = (f32[64,256]{1,0:T(8,128)}, f32[256,64]{0,1:T(8,128)}) async-done(((f32[64,256]{1,0:T(8,128)}, f32[256,64]{0,1:T(8,128)}), (f32[64,256]{1,0:T(8,128)}, f32[256,64]{0,1:T(8,128)})) %all-reduce.12.cloned.1.call-update) | async-done | bytes 131088 | tf_op jit(solution)/shard_map/psum | solution.py:238
  125.9 1.5 broadcast_multiply_fusion.1
  127.3 1.5 broadcast_multiply_fusion
  128.8 17.8 %all-reduce.10.cloned.1.call-done = f32[1024,128]{1,0:T(8,128)} async-done(((f32[1024,128]{1,0:T(8,128)}), f32[1024,128]{1,0:T(8,128)}) %all-reduce.10.cloned.1.call-update) | async-done | bytes 524304 | tf_op jit(solution)/shard_map/psum | solution.py:181
  146.6 1.8 multiply_reduce_fusion
  148.5 0.6 multiply_convert_fusion.1
  150.6 5.9 %fusion.19 = f32[1,38,38,128]{3,1,2,0:T(8,128)S(1)} fusion(f32[1,44,44,128]{3,1,2,0:T(8,128)S(1)} %pad_convert_fusion, f32[128]{0:T(128)S(1)} %get-tuple-element.418, f32[128]{0:T(128)S(1)} %get-tuple-element.419, f32[128]{0:T(128)S(1)} %get-tuple-element.372, f32[128]{0:T(128)S(1)} %get-tuple-element.373, f32[128]{0:T(128)S(1)} %get-tuple-element.374, ...), kind=kLoop, calls=%fused_computation.114 | loop fusion | flops 17928704 | bytes 36991488 | tf_op jit(solution)/shard_map/add | solution.py:107
  156.8 13.5 %all-gather.2 = f32[16,1,3,3,128]{4,1,3,2,0:T(1,128)S(1)} all-gather(f32[4,1,3,3,128]{4,1,3,2,0:T(1,128)S(1)} %copy.86), channel_id=4, replica_groups=mesh['group'=2,'tile'=4,'dp'=2,'chan'=2] {'tile'}, dimensions={0}, use_global_device_ids=true | all-gather | bytes 92160 | tf_op jit(solution)/shard_map/all_gather | solution.py:209
  170.5 17.8 %all-gather.1 = f32[16,1,3,32,128]{4,3,2,1,0:T(8,128)S(1)} all-gather(f32[4,1,3,32,128]{4,3,2,1,0:T(8,128)S(1)} %pad_maximum_fusion.2), channel_id=3, replica_groups=mesh['group'=2,'tile'=4,'dp'=2,'chan'=2] {'tile'}, dimensions={0}, use_global_device_ids=true | all-gather | bytes 983040 | tf_op jit(solution)/shard_map/all_gather | solution.py:208
  188.3 60.0 %while.19 = (s32[]{:T(128)}, f32[4,1,3,32,128]{4,3,2,1,0:T(8,128)S(1)}, s32[4,8,2]{1,2,0:T(2,128)S(1)}, s32[]{:T(128)}, f32[4,4,1,3,32,128]{5,4,3,2,1,0:T(8,128)...) while((s32[]{:T(128)}, ...), condition=%wide.region_6.7_spmd, body=%wide.region_5.6_spmd.sunk | while | flops 196738 | bytes 1476261 | solution.py:228
  188.3 0.7 constant_dynamic-slice_fusion.47
  203.3 0.7 constant_dynamic-slice_fusion.47
  218.3 0.7 constant_dynamic-slice_fusion.47
  233.3 0.7 constant_dynamic-slice_fusion.47
  248.6 57.7 %all-reduce.5 = (f32[49,128]{1,0:T(8,128)S(1)}, f32[128]{0:T(128)S(1)}, f32[128]{0:T(128)S(1)}) all-reduce(f32[49,128]{1,0:T(8,128)S(1)} %stack.259, f32[128]{0:T(128)S(1)} %get-tuple-element.252, f32[128]{0:T(128)S(1)} %fusion.13), channel_id=1, replica_groups=mesh['group'=2,'tile'=4,'dp'=2,'chan'=2] {'tile','dp','chan'}, use_global_device_ids=true, to_apply=%region_56.57 | all-reduce | flops 6528 | bytes 52224 | tf_op jit(solution)/shard_map/psum | solution.py:235
  306.3 0.6 broadcast_multiply_fusion.2
  306.9 0.5 broadcast_multiply_fusion.7
  308.7 0.8 copy.92
  (157 shorter events, 9.0 us)
Async XLA Ops:
  7.2 54.5 %copy-start = (bf16[128,256]{1,0:T(8,128)(2,1)S(1)}, bf16[128,256]{1,0:T(8,128)(2,1)}, u32[]{:S(2)}) copy-start(bf16[128,256]{1,0:T(8,128)(2,1)} %param.21) | copy-start | bytes 196612
  7.2 69.2 %reduce-scatter.3.cloned.1.call-start = ((), (), s32[]{:S(2)}) async-start(), calls=%async_computation.3 | async-start | bytes 196608 | tf_op jit(solution)/shard_map/reduce_scatter | solution.py:240
  59.6 1.0 copy-start.3
  60.6 0.7 copy-start.7
  60.6 0.7 copy-start.6
  61.7 0.8 copy-start.5
  64.2 24.7 %reduce-scatter.5.cloned.1.call-start = ((), (), s32[]{:S(2)}) async-start(), calls=%async_computation.4 | async-start | bytes 196608 | tf_op jit(solution)/shard_map/reduce_scatter | solution.py:241
  65.2 60.6 %all-reduce.12.cloned.1.call-start = ((), (), s32[]{:S(2)}) async-start(), calls=%async_computation.5 | async-start | bytes 262144 | tf_op jit(solution)/shard_map/psum | solution.py:238
  88.9 57.7 %all-reduce.10.cloned.1.call-start = ((), (), s32[]{:S(2)}) async-start(), calls=%async_computation.2 | async-start | bytes 1048576 | tf_op jit(solution)/shard_map/psum | solution.py:181
  90.3 56.4 %copy-start.1 = (f32[1024,128]{1,0:T(8,128)S(1)}, f32[1024,128]{1,0:T(8,128)}, u32[]{:S(2)}) copy-start(f32[1024,128]{1,0:T(8,128)} %fusion.138) | copy-start | bytes 1572868
  146.6 1.8 copy-start.2
  170.4 17.9 %copy-start.4 = (s32[4,8,2]{1,2,0:T(2,128)S(1)}, s32[4,8,2]{1,2,0:T(2,128)}, u32[]{:S(2)}) copy-start(s32[4,8,2]{1,2,0:T(2,128)} %param.25) | copy-start | bytes 772
Sparse Core Ops, SparseCore 0:
  64.4 11.9 reduce-scatter.2
  78.6 10.2 reduce-scatter.4
  91.3 34.5 all-reduce.11
  128.2 18.4 all-reduce.9
where the time goes:
time: 318 us; the launch traced here: 316 us
  blocking collectives  105 us (33%)
  waiting for transfers between devices  75.9 us (24%)
  loops' own time  56.3 us (18%)
  between operations  38.5 us (12%)
  other arithmetic  21.8 us (7%)
  local copies, waits for them, and re-layouts  13.4 us (4%)
  matrix products  4.59 us (1%)
    psum x1, blocking collectives, on_device(): lax.psum((kernel_part, gain_part, scale_part), ('tile', 'dp', 'chan'))  57.7 us
    another operation x1, loops' own time, on_device(): incoming = lax.fori_loop(0, edge_shards.shape[0], per_tile, collected)  56.3 us
    psum x1, waiting for transfers between devices, on_device(): w_in_tile, w_out_tile = lax.psum((w_in_part, w_out_part), 'tile')  34.4 us
    psum x1, waiting for transfers between devices, on_device(): lax.psum(rows_part, 'chan')  17.8 us
    all_gather x1, blocking collectives, on_device(): edge_shards = lax.all_gather(edge_slots[None], 'tile', axis=0, tiled=True)  17.8 us
    all_gather x1, blocking collectives, on_device(): shards = lax.all_gather(faces_out[None], 'tile', axis=0, tiled=True)  16.2 us
    all_gather x1, blocking collectives, on_device(): lax.all_gather(corner_slots[None], 'tile', axis=0, tiled=True)  13.5 us
    reduce_scatter x1, waiting for transfers between devices, on_device(): lax.psum_scatter(w_out_tile, 'dp', scatter_dimension=1, tiled=True)  12.5 us
  transfers between devices with their start and end apart: 4, of which 4 were waited for; matrix products, arithmetic and copies ran while one was open for 2% of the time, Pallas kernels for 0%

commit v1 on v0

v1 whole, which is shorter than its diff:
```python
import functools
import math

import jax
import jax.numpy as jnp
from jax import lax
from jax.experimental import pallas as pl
from jax.experimental.pallas import tpu as pltpu
from jax.sharding import PartitionSpec as P

KS = 7
H = KS // 2
COL = 8
ROWS_AT_ONCE = 4
SMALL_ROWS = 56

eps = 1e-06
root_two_pi = 0.7978845608028654
cubic_coef = 0.044715
facing_turns = (2, 3, 0, 1, 2, 0, 0, 2)
corner_at_end = (True, False, True, False)
MESH = pl.DeviceIdType.MESH
F32 = jnp.float32
BF16 = jnp.bfloat16


def gelu_pair(values):
    square = values * values
    tanh_part = jnp.tanh(values * (root_two_pi + (root_two_pi * cubic_coef) * square))
    half_up = 0.5 + 0.5 * tanh_part
    active = values * half_up
    gelu_slope = half_up + active * (1.0 - tanh_part) * (
        root_two_pi + (3.0 * root_two_pi * cubic_coef) * square
    )
    return active, gelu_slope


def mm(left, right, left_dim, right_dim):
    return lax.dot_general(
        left, right, (((left_dim,), (right_dim,)), ((), ())), preferred_element_type=F32
    )


def body(
    tiles, dps, factor,
    adj, x_ref, ct_ref, kern, gain_ref, w_in_ref, w_out_ref, scale_ref,
    out_ref, small_out, w_out_all,
    pad, strips, faces, win, wout, conv_ref, part, cg, cpad, gpad, rimf, rims, incoming,
    chan_recv, dp_send, dp_recv, tile_grads, kacc, small_chan, small_dp, small_tile, base,
    face_send, face_recv, pair_send, pair_recv, rim_send, rim_recv,
    dp_send_sem, dp_recv_sem, tg_send, tg_recv, sd_send, sd_recv, st_send, st_recv,
):
    ts = x_ref.shape[0]
    half = ts // 2
    strip = H * ts
    me_t = lax.axis_index("tile")
    me_d = lax.axis_index("dp")
    me_c = lax.axis_index("chan")
    sib = 1 - me_c

    barrier = pltpu.get_barrier_semaphore()
    for o in range(1, tiles):
        pl.semaphore_signal(barrier, inc=1, device_id={"tile": lax.rem(me_t + o, tiles)}, device_id_type=MESH)
    for o in range(1, dps):
        pl.semaphore_signal(barrier, inc=1, device_id={"dp": lax.rem(me_d + o, dps)}, device_id_type=MESH)
    pl.semaphore_signal(barrier, inc=1, device_id={"chan": sib}, device_id_type=MESH)

    def to_peers(axis, size, me, source, target, send_sems, recv_sems):
        copies = []
        for o in range(1, size):
            peer = lax.rem(me + o, size)
            copy = pltpu.make_async_remote_copy(
                src_ref=source(peer), dst_ref=target, send_sem=send_sems.at[o - 1],
                recv_sem=recv_sems.at[o - 1], device_id={axis: peer}, device_id_type=MESH,
            )
            copy.start()
            copies.append(copy)
        return copies

    def to_sibling(source, target, index):
        copy = pltpu.make_async_remote_copy(
            src_ref=source, dst_ref=target, send_sem=pair_send.at[index],
            recv_sem=pair_recv.at[index], device_id={"chan": sib}, device_id_type=MESH,
        )
        copy.start()
        return copy

    def rows_loop(count, step):
        def wrapped(index, carry):
            step(index)
            return carry
        lax.fori_loop(0, count, wrapped, 0)

    def fill(i):
        pad[H + i, COL:COL + ts, :] = x_ref[i].astype(F32)
    rows_loop(ts, fill)
    for d in range(H):
        strips[0, d * ts:(d + 1) * ts, :] = x_ref[d].astype(F32)

    def face_row(p):
        for d in range(H):
            strips[1, pl.ds(d * ts + p, 1), :] = pad[H + p, COL + ts - 1 - d:COL + ts - d, :]
            strips[2, pl.ds(d * ts + p, 1), :] = pad[H + ts - 1 - d, pl.ds(COL + ts - 1 - p, 1), :]
            strips[3, pl.ds(d * ts + p, 1), :] = pad[H + ts - 1 - p, COL + d:COL + d + 1, :]
    rows_loop(ts, face_row)
    for f in range(4):
        faces[me_t, f] = strips[f].astype(BF16)
    win[me_c] = w_in_ref[...]
    wout[me_c] = w_out_ref[...]

    pl.semaphore_wait(barrier, tiles - 1 + dps - 1 + 1)
    face_copies = to_peers("tile", tiles, me_t, lambda peer: faces.at[me_t], faces.at[me_t], face_send, face_recv)
    win_copy = to_sibling(win.at[me_c], win.at[me_c], 0)
    wout_copy = to_sibling(wout.at[me_c], wout.at[me_c], 1)

    def zero_rows(i):
        cpad[i] = jnp.zeros(cpad.shape[1:], F32)
    rows_loop(cpad.shape[0], zero_rows)
    kacc[...] = jnp.zeros_like(kacc)

    for copy in face_copies:
        copy.wait_recv()

    for k in range(8):
        source = adj[me_t, k, 0]
        face = (adj[me_t, k, 1] + facing_turns[k]) % 4
        strips[k] = faces[source, face].astype(F32)
    for d in range(H):
        pad[H + ts + d, COL:COL + ts, :] = strips[2, d * ts:(d + 1) * ts, :]

    def rim_row(p):
        for d in range(H):
            pad[d, pl.ds(COL + p, 1), :] = strips[0, pl.ds((H - 1 - d) * ts + ts - 1 - p, 1), :]
            pad[H + p, COL + ts + d:COL + ts + d + 1, :] = strips[1, pl.ds(d * ts + ts - 1 - p, 1), :]
            pad[H + p, COL - H + d:COL - H + d + 1, :] = strips[3, pl.ds((H - 1 - d) * ts + p, 1), :]
    rows_loop(ts, rim_row)
    for i in range(H):
        for j in range(H):
            at = (H - 1 - i) * ts + ts - H + (H - 1 - j)
            pad[i, COL + ts + j:COL + ts + j + 1, :] = strips[4, at:at + 1, :]
            at = i * ts + j
            pad[H + ts + i, COL + ts + j:COL + ts + j + 1, :] = strips[5, at:at + 1, :]
            at = i * ts + ts - H + j
            pad[H + ts + i, COL - H + j:COL - H + j + 1, :] = strips[6, at:at + 1, :]
            at = (H - 1 - i) * ts + (H - 1 - j)
            pad[i, COL - H + j:COL - H + j + 1, :] = strips[7, at:at + 1, :]

    first = me_c * half

    def conv_rows(block):
        i = block * ROWS_AT_ONCE
        acc = [jnp.zeros((ts, pad.shape[2]), F32) for _ in range(ROWS_AT_ONCE)]
        for a in range(ROWS_AT_ONCE + KS - 1):
            for b in range(KS):
                window = pad[first + i + a, COL - H + b:COL - H + b + ts, :]
                for r in range(ROWS_AT_ONCE):
                    if 0 <= a - r < KS:
                        at = (a - r) * KS + b
                        acc[r] = acc[r] + window * kern[at:at + 1, :]
        for r in range(ROWS_AT_ONCE):
            conv_ref[i + r] = acc[r]
    rows_loop(half // ROWS_AT_ONCE, conv_rows)

    win_copy.wait_recv()
    wout_copy.wait_recv()

    gain = gain_ref[...]
    layer_scale = scale_ref[...]
    block_rows = 8
    pixels = block_rows * ts
    channels = pad.shape[2]
    gain_total = jnp.zeros((1, channels), F32)
    scale_total = jnp.zeros((1, channels), F32)
    for block in range(half // block_rows):
        at = block * block_rows
        conv = conv_ref[at:at + block_rows].reshape(pixels, channels)
        mean = jnp.mean(conv, axis=1, keepdims=True)
        centred = conv - mean
        inv_std = lax.rsqrt(jnp.mean(centred * centred, axis=1, keepdims=True) + eps)
        normed = centred * inv_std
        normed_b = (normed * gain).astype(BF16)
        upstream = ct_ref[pl.ds(first + at, block_rows)].reshape(pixels, channels).astype(F32)
        scaled_b = (upstream * layer_scale).astype(BF16)
        branch = jnp.zeros((pixels, channels), F32)
        normed_grad = jnp.zeros((pixels, channels), F32)
        for c in range(2):
            active, slope = gelu_pair(mm(normed_b, win[c], 1, 0))
            active_b = active.astype(BF16)
            branch = branch + mm(active_b, wout[c], 1, 0)
            hidden_grad = (mm(scaled_b, wout[c], 1, 1) * slope).astype(BF16)
            normed_grad = normed_grad + mm(hidden_grad, win[c], 1, 1)
            in_grad = mm(normed_b, hidden_grad, 0, 0)
            out_grad = mm(scaled_b, active_b, 0, 0)
            if block == 0:
                part[c, 0] = in_grad
                part[c, 1] = out_grad
            else:
                part[c, 0] += in_grad
                part[c, 1] += out_grad
        scale_total = scale_total + jnp.sum(upstream * branch, axis=0, keepdims=True)
        gain_total = gain_total + jnp.sum(normed_grad * normed, axis=0, keepdims=True)
        scaled = normed_grad * gain
        first_mean = jnp.mean(scaled, axis=1, keepdims=True)
        second_mean = jnp.mean(scaled * normed, axis=1, keepdims=True)
        grad_b = (inv_std * (scaled - first_mean - normed * second_mean)).astype(BF16)
        cg[pl.ds(first + at, block_rows)] = grad_b.reshape(block_rows, ts, channels)

    cg_copy = to_sibling(cg.at[pl.ds(first, half)], cg.at[pl.ds(first, half)], 2)
    part_copy = to_sibling(part.at[sib], chan_recv, 3)

    for a in range(KS):
        def kernel_row(i, acc):
            grad = cg[first + i].astype(F32)
            new = []
            for b in range(KS):
                window = pad[first + i + a, COL - H + b:COL - H + b + ts, :]
                new.append(acc[b] + jnp.sum((window * grad).reshape(ts // 8, 8, channels), axis=0))
            return tuple(new)
        sums = lax.fori_loop(0, half, kernel_row, tuple(jnp.zeros((8, channels), F32) for _ in range(KS)))
        for b in range(KS):
            kacc[a * KS + b] = sums[b]
    small_chan[0] = jnp.sum(kacc[...], axis=1)
    small_chan[0, KS * KS:KS * KS + 1, :] = gain_total
    small_chan[0, KS * KS + 1:KS * KS + 2, :] = scale_total
    small_copy = to_sibling(small_chan.at[0], small_chan.at[1], 4)

    cg_copy.wait_recv()

    def widen(i):
        cpad[KS - 1 + i, COL:COL + ts, :] = cg[i].astype(F32)
    rows_loop(ts, widen)
    wide = gpad.shape[1]

    def spread_rows(block):
        i = block * 2
        acc = [jnp.zeros((wide, channels), F32) for _ in range(2)]
        for a in range(KS + 1):
            for b in range(KS):
                window = cpad[i + a, COL - (KS - 1) + b:COL - (KS - 1) + b + wide, :]
                for r in range(2):
                    if 0 <= a - r < KS:
                        at = (KS - 1 - (a - r)) * KS + KS - 1 - b
                        acc[r] = acc[r] + window * kern[at:at + 1, :]
        for r in range(2):
            gpad[i + r] = acc[r]
    rows_loop((ts + 2 * H) // 2, spread_rows)

    def edge_row(p):
        for d in range(H):
            rimf[pl.ds(d * ts + p, 1), :] = gpad[H - 1 - d, pl.ds(H + ts - 1 - p, 1), :]
            rimf[pl.ds(strip + d * ts + p, 1), :] = gpad[H + ts - 1 - p, H + ts + d:H + ts + d + 1, :]
            rimf[pl.ds(3 * strip + d * ts + p, 1), :] = gpad[H + p, H - 1 - d:H - d, :]
    rows_loop(ts, edge_row)
    rimf[4 * strip:, :] = jnp.zeros((64, channels), F32)
    for d in range(H):
        rimf[2 * strip + d * ts:2 * strip + (d + 1) * ts, :] = gpad[H + ts + d, H:H + ts, :]
    for i in range(H):
        for j in range(H):
            spots = (
                (H - 1 - i, H + ts + H - 1 - j), (H + ts + i, H + ts + j),
                (H + ts + i, j), (H - 1 - i, H - 1 - j),
            )
            for k in range(4):
                at = 4 * strip + 16 * k + H * i + j
                row, col = spots[k]
                rimf[at:at + 1, :] = gpad[row, col:col + 1, :]
    rims[me_t] = rimf[...].astype(BF16)
    rim_copies = to_peers("tile", tiles, me_t, lambda peer: rims.at[me_t], rims.at[me_t], rim_send, rim_recv)

    part_rows = channels // dps
    part_copy.wait_recv()
    for w in range(2):
        for d in range(dps):
            rows = slice(d * part_rows, (d + 1) * part_rows)
            dp_send[d, w] = part[me_c, w, rows, :] + chan_recv[w, rows, :]
    dp_recv[me_d] = dp_send[me_d]
    dp_copies = to_peers("dp", dps, me_d, lambda peer: dp_send.at[peer], dp_recv.at[me_d], dp_send_sem, dp_recv_sem)
    small_copy.wait_recv()
    small_dp[me_d] = small_chan[0] + small_chan[1]
    sd_copies = to_peers("dp", dps, me_d, lambda peer: small_dp.at[me_d], small_dp.at[me_d], sd_send, sd_recv)

    def base_row(i):
        base[i] = ct_ref[i].astype(F32) + gpad[H + i, H:H + ts, :]
    rows_loop(ts, base_row)

    for copy in dp_copies:
        copy.wait_recv()
    total = dp_recv[0]
    for d in range(1, dps):
        total = total + dp_recv[d]
    tile_grads[me_t] = total.astype(tile_grads.dtype)
    tg_copies = to_peers("tile", tiles, me_t, lambda peer: tile_grads.at[me_t], tile_grads.at[me_t], tg_send, tg_recv)
    for copy in sd_copies:
        copy.wait_recv()
    total = small_dp[0]
    for d in range(1, dps):
        total = total + small_dp[d]
    small_tile[me_t] = total
    st_copies = to_peers("tile", tiles, me_t, lambda peer: small_tile.at[me_t], small_tile.at[me_t], st_send, st_recv)

    for copy in rim_copies:
        copy.wait_recv()
    for f in range(4):
        def gather(p, carry):
            edge, at_start, at_end = carry
            for k in range(8):
                face = (adj[p, k, 1] + facing_turns[k]) % 4
                chosen = jnp.where((adj[p, k, 0] == me_t) & (face == f), 1.0, 0.0).astype(F32)
                if k < 4:
                    edge = edge + chosen * rims[p, strip * k:strip * (k + 1), :].astype(F32)
                else:
                    at = 4 * strip + 16 * (k - 4)
                    piece = chosen * rims[p, at:at + 16, :].astype(F32)
                    if corner_at_end[k - 4]:
                        at_end = at_end + piece
                    else:
                        at_start = at_start + piece
            return edge, at_start, at_end
        zero = jnp.zeros((16, channels), F32)
        edge, at_start, at_end = lax.fori_loop(0, tiles, gather, (jnp.zeros((strip, channels), F32), zero, zero))
        incoming[f] = edge
        for d in range(H):
            incoming[f, d * ts:d * ts + H, :] += at_start[d * H:(d + 1) * H]
            incoming[f, (d + 1) * ts - H:(d + 1) * ts, :] += at_end[d * H:(d + 1) * H]
    for d in range(H):
        base[d] += incoming[0, d * ts:(d + 1) * ts, :]

    def add_row(p):
        for d in range(H):
            base[p, ts - H + d:ts - H + d + 1, :] += incoming[1, pl.ds((H - 1 - d) * ts + p, 1), :]
            base[ts - H + d, pl.ds(p, 1), :] += incoming[2, pl.ds((H - 1 - d) * ts + ts - 1 - p, 1), :]
            base[p, d:d + 1, :] += incoming[3, pl.ds(d * ts + ts - 1 - p, 1), :]
    rows_loop(ts, add_row)

    def out_row(i):
        out_ref[i] = base[i].astype(BF16)
    rows_loop(ts, out_row)

    for copy in tg_copies:
        copy.wait_recv()
    total = tile_grads[0].astype(F32)
    for t in range(1, tiles):
        total = total + tile_grads[t].astype(F32)
    w_out_all[...] = total * factor
    for copy in st_copies:
        copy.wait_recv()
    total = small_tile[0]
    for t in range(1, tiles):
        total = total + small_tile[t]
    small_out[...] = total * factor

    for copy in face_copies + rim_copies + dp_copies + sd_copies + tg_copies + st_copies + [
        win_copy, wout_copy, cg_copy, part_copy, small_copy
    ]:
        copy.wait_send()


def on_device(inputs, kernel, norm_gain, w_in, w_out, layer_scale, cotangent, adjacency):
    ts, ch = inputs.shape[2], inputs.shape[4]
    hid = w_in.shape[1]
    tiles, dps = lax.axis_size("tile"), lax.axis_size("dp")
    factor = 1.0 / math.sqrt(dps * tiles * ts * ts)
    strip = H * ts
    rim_rows = 4 * strip + 64
    part_rows = ch // dps
    vmem = pl.BlockSpec(memory_space=pltpu.VMEM)
    dma = pltpu.SemaphoreType.DMA
    peers_t, peers_d = max(tiles - 1, 1), max(dps - 1, 1)
    out, small, grads = pl.pallas_call(
        functools.partial(body, tiles, dps, factor),
        out_shape=(
            jax.ShapeDtypeStruct((ts, ts, ch), BF16),
            jax.ShapeDtypeStruct((SMALL_ROWS, ch), F32),
            jax.ShapeDtypeStruct((2, part_rows, hid), F32),
        ),
        in_specs=[pl.BlockSpec(memory_space=pltpu.SMEM)] + [vmem] * 7,
        out_specs=(vmem,) * 3,
        scratch_shapes=[
            pltpu.VMEM((ts + 2 * H, ts + 2 * COL, ch), F32),
            pltpu.VMEM((8, strip, ch), F32),
            pltpu.VMEM((tiles, 4, strip, ch), BF16),
            pltpu.VMEM((2, ch, hid), BF16),
            pltpu.VMEM((2, hid, ch), BF16),
            pltpu.VMEM((ts // 2, ts, ch), F32),
            pltpu.VMEM((2, 2, ch, hid), F32),
            pltpu.VMEM((ts, ts, ch), BF16),
            pltpu.VMEM((ts + 2 * (KS - 1), ts + 2 * COL, ch), F32),
            pltpu.VMEM((ts + 2 * H, ts + 8, ch), F32),
            pltpu.VMEM((rim_rows, ch), F32),
            pltpu.VMEM((tiles, rim_rows, ch), BF16),
            pltpu.VMEM((4, strip, ch), F32),
            pltpu.VMEM((2, ch, hid), F32),
            pltpu.VMEM((dps, 2, part_rows, hid), F32),
            pltpu.VMEM((dps, 2, part_rows, hid), F32),
            pltpu.VMEM((tiles, 2, part_rows, hid), BF16),
            pltpu.VMEM((SMALL_ROWS, 8, ch), F32),
            pltpu.VMEM((2, SMALL_ROWS, ch), F32),
            pltpu.VMEM((dps, SMALL_ROWS, ch), F32),
            pltpu.VMEM((tiles, SMALL_ROWS, ch), F32),
            pltpu.VMEM((ts, ts, ch), F32),
            dma((peers_t,)), dma((peers_t,)), dma((5,)), dma((5,)), dma((peers_t,)), dma((peers_t,)),
            dma((peers_d,)), dma((peers_d,)), dma((peers_t,)), dma((peers_t,)),
            dma((peers_d,)), dma((peers_d,)), dma((peers_t,)), dma((peers_t,)),
        ],
        compiler_params=pltpu.CompilerParams(
            collective_id=0, has_side_effects=True, vmem_limit_bytes=48 * 1024 * 1024
        ),
    )(
        adjacency, inputs[0, 0], cotangent[0, 0], kernel, norm_gain[None], w_in, w_out, layer_scale[None]
    )
    taps = KS * KS
    return (
        out[None, None],
        small[:taps],
        small[taps],
        grads[0],
        grads[1].T,
        small[taps + 1],
    )


def solution(mesh):
    placed = (
        P(("group", "dp"), "tile", None, None, None),
        P(),
        P(),
        P(None, "chan"),
        P("chan", None),
        P(),
        P(("group", "dp"), "tile", None, None, None),
        P(),
    )
    return jax.shard_map(
        on_device,
        mesh=mesh,
        in_specs=placed,
        out_specs=(
            P(("group", "dp"), "tile", None, None, None),
            P("group", None),
            P("group"),
            P(("group", "dp"), "chan"),
            P(("group", "chan"), "dp"),
            P("group"),
        ),
        check_vma=False,
    )
```

time: 318 us -> 51.6 us (0.16)
  blocking collectives: 105 us -> 0 us
  waiting for transfers between devices: 75.9 us -> 0 us
  loops' own time: 56.3 us -> 0 us
  Pallas kernels: 0 us -> 42.4 us
  between operations: 38.5 us -> 0.66 us
  other arithmetic: 21.8 us -> 0 us
  local copies, waits for them, and re-layouts: 13.4 us -> 8.16 us
  matrix products: 4.59 us -> 0 us
    psum x1 -> x0, blocking collectives: 57.7 us -> none  [on_device(): lax.psum((kernel_part, gain_part, scale_part), ('tile', 'dp', 'chan'))]
    another operation x1 -> x0, loops' own time: 56.3 us -> none  [on_device(): incoming = lax.fori_loop(0, edge_shards.shape[0], per_tile, collected)]
    psum x2 -> x0, waiting for transfers between devices: 52.3 us -> none  [the longest x1 34.4 us: on_device(): w_in_tile, w_out_tile = lax.psum((w_in_part, w_out_part), 'tile')]
    all_gather x3 -> x0, blocking collectives: 47.5 us -> none  [the longest x1 17.8 us: on_device(): edge_shards = lax.all_gather(edge_slots[None], 'tile', axis=0, tiled=True)]
    pallas_call x0 -> x1, Pallas kernels: none -> 42.4 us  [on_device(): pl.pallas_call(functools.partial(body, tiles, dps, factor), out_shape=(ja...]
    reduce_scatter x2 -> x0, waiting for transfers between devices: 23.6 us -> none  [the longest x1 12.5 us: on_device(): lax.psum_scatter(w_out_tile, 'dp', scatter_dimension=1, tiled=True)]
    reduce_sum x6 -> x0, other arithmetic: 8.21 us -> none  [the longest x1 4.69 us: norm_forward(): row_mean = jnp.mean(conv_flat, axis=1, keepdims=True)]
    add x4 -> x0, other arithmetic: 6.07 us -> none  [the longest x1 5.87 us: spread_back(): summed = summed + kernel[shift_row * KS + shift_col] * window]
  transfers between devices with their start and end apart: 4 -> 0, of which waited for: 4 -> 0; matrix products, arithmetic and copies ran while one was open for 2% -> 0% of each run, Pallas kernels for 0% -> 0%
where the time goes in v1:
time: 51.6 us; the launch traced here: 51.2 us
  Pallas kernels  42.4 us (82%)
  local copies, waits for them, and re-layouts  8.16 us (16%)
  between operations  0.66 us (1%)
    pallas_call x1, Pallas kernels, on_device(): pl.pallas_call(functools.partial(body, tiles, dps, factor), out_shape=(ja...  42.4 us
    unnamed x19, local copies, waits for them, and re-layouts  6.98 us

profile of v1, /device:TPU:0, one launch (start us, length us, event | category | flops | bytes accessed | tf_op | source)
XLA Modules:
  0.0 51.2 jit_solution(17215700412175386164)
XLA Ops:
  0.6 0.0 copy-start.7
  0.6 0.7 %copy-done.7 = s32[4,8,2]{1,2,0:T(2,128)S(1)} copy-done((s32[4,8,2]{1,2,0:T(2,128)S(1)}, s32[4,8,2]{1,2,0:T(2,128)}, u32[]{:S(2)}) %copy-start.7) | copy-done | bytes 280
  1.3 0.0 copy-start.5
  1.3 0.0 copy-start.6
  1.3 0.1 copy.14.adj
  1.4 0.6 %copy-done.5 = f32[128]{0:T(128)S(1)} copy-done((f32[128]{0:T(128)S(1)}, f32[128]{0:T(128)}, u32[]{:S(2)}) %copy-start.5) | copy-done | bytes 536
  2.0 0.0 copy-done.6
  2.0 0.0 copy-start
  2.0 0.9 %copy-done = bf16[1,1,32,32,128]{4,3,2,1,0:T(8,128)(2,1)S(1)} copy-done((bf16[1,1,32,32,128]{4,3,2,1,0:T(8,128)(2,1)S(1)}, bf16[1,1,32,32,128]{4,3,2,1,0:T(8,128)(2,1)}, u32[]{:S(2)}) %copy-start) | copy-done | bytes 262168
  2.9 0.0 copy-start.1
  2.9 0.9 %copy-done.1 = bf16[1,1,32,32,128]{4,3,2,1,0:T(8,128)(2,1)S(1)} copy-done((bf16[1,1,32,32,128]{4,3,2,1,0:T(8,128)(2,1)S(1)}, bf16[1,1,32,32,128]{4,3,2,1,0:T(8,128)(2,1)}, u32[]{:S(2)}) %copy-start.1) | copy-done | bytes 262168
  3.9 0.0 copy-start.2
  3.9 0.8 %copy-done.2 = bf16[128,256]{1,0:T(8,128)(2,1)S(1)} copy-done((bf16[128,256]{1,0:T(8,128)(2,1)S(1)}, bf16[128,256]{1,0:T(8,128)(2,1)}, u32[]{:S(2)}) %copy-start.2) | copy-done | bytes 65560
  4.7 0.0 copy-start.3
  4.7 0.8 %copy-done.3 = bf16[256,128]{1,0:T(8,128)(2,1)S(1)} copy-done((bf16[256,128]{1,0:T(8,128)(2,1)S(1)}, bf16[256,128]{1,0:T(8,128)(2,1)}, u32[]{:S(2)}) %copy-start.3) | copy-done | bytes 65560
  5.6 0.0 copy-start.4
  5.6 0.7 %copy-done.4 = f32[49,128]{1,0:T(8,128)S(1)} copy-done((f32[49,128]{1,0:T(8,128)S(1)}, f32[49,128]{1,0:T(8,128)}, u32[]{:S(2)}) %copy-start.4) | copy-done | bytes 25112
  6.3 42.4 %shard_map.127 = (bf16[32,32,128]{2,1,0:T(8,128)(2,1)S(1)}, f32[56,128]{1,0:T(8,128)S(1)}, f32[2,64,256]{2,1,0:T(8,128)S(1)}) custom-call(s32[4,8,2]{2,1,0:T(8,128)S(1)} %copy.14.adj, bf16[32,32,128]{2,1,0:T(8,128)(2,1)S(1)} %bitcast.16, bf16[32,32,128]{2,1,0:T(8,128)(2,1)S(1)} %bitcast.17, f32[49,128]{1,0:T(8,128)S(1)} %copy-done.4, f32[1,128]{1,0:T(1,128)S(1)} %bitcast.20, ...), custom_call_target="tpu_custom_call" | custom-call | tf_op jit(solution)/shard_map/pallas_call | solution.py:369
  48.8 0.5 %slice_bitcast_fusion.2 = (f32[128]{0:T(128)}, f32[128]{0:T(128)}) fusion(f32[56,128]{1,0:T(8,128)S(1)} %get-tuple-element.10), kind=kLoop, calls=%fused_computation.2 | loop fusion | bytes 2048 | tf_op jit(solution)/shard_map/squeeze | solution.py:418
  49.3 0.7 %slice_bitcast_fusion = (f32[256,64]{0,1:T(8,128)}, f32[64,256]{1,0:T(8,128)}) fusion(f32[2,64,256]{2,1,0:T(8,128)S(1)} %get-tuple-element.11), kind=kLoop, calls=%fused_computation | loop fusion | bytes 262144 | tf_op jit(solution)/shard_map/transpose | solution.py:417
  49.9 0.7 %copy.17 = bf16[1,1,32,32,128]{4,3,2,1,0:T(8,128)(2,1)} copy(bf16[1,1,32,32,128]{4,3,2,1,0:T(8,128)(2,1)S(1)} %bitcast.18) | data formatting | bytes 524288
  50.6 0.6 %copy.18 = f32[49,128]{1,0:T(8,128)} copy(f32[49,128]{1,0:T(8,128)S(1)} %bitcast.19) | data formatting | bytes 50176
Async XLA Ops:
  0.6 0.7 %copy-start.7 = (s32[4,8,2]{1,2,0:T(2,128)S(1)}, s32[4,8,2]{1,2,0:T(2,128)}, u32[]{:S(2)}) copy-start(s32[4,8,2]{1,2,0:T(2,128)} %param.15) | copy-start | bytes 772
  1.3 0.7 %copy-start.5 = (f32[128]{0:T(128)S(1)}, f32[128]{0:T(128)}, u32[]{:S(2)}) copy-start(f32[128]{0:T(128)} %param.10) | copy-start | bytes 1540
  1.3 0.7 %copy-start.6 = (f32[128]{0:T(128)S(1)}, f32[128]{0:T(128)}, u32[]{:S(2)}) copy-start(f32[128]{0:T(128)} %param.13) | copy-start | bytes 1540
  2.0 0.9 %copy-start = (bf16[1,1,32,32,128]{4,3,2,1,0:T(8,128)(2,1)S(1)}, bf16[1,1,32,32,128]{4,3,2,1,0:T(8,128)(2,1)}, u32[]{:S(2)}) copy-start(bf16[1,1,32,32,128]{4,3,2,1,0:T(8,128)(2,1)} %param.8) | copy-start | bytes 786436
  2.9 0.9 %copy-start.1 = (bf16[1,1,32,32,128]{4,3,2,1,0:T(8,128)(2,1)S(1)}, bf16[1,1,32,32,128]{4,3,2,1,0:T(8,128)(2,1)}, u32[]{:S(2)}) copy-start(bf16[1,1,32,32,128]{4,3,2,1,0:T(8,128)(2,1)} %param.14) | copy-start | bytes 786436
  3.9 0.8 %copy-start.2 = (bf16[128,256]{1,0:T(8,128)(2,1)S(1)}, bf16[128,256]{1,0:T(8,128)(2,1)}, u32[]{:S(2)}) copy-start(bf16[128,256]{1,0:T(8,128)(2,1)} %w_in_ref.1) | copy-start | bytes 196612
  4.7 0.8 %copy-start.3 = (bf16[256,128]{1,0:T(8,128)(2,1)S(1)}, bf16[256,128]{1,0:T(8,128)(2,1)}, u32[]{:S(2)}) copy-start(bf16[256,128]{1,0:T(8,128)(2,1)} %w_out_ref.1) | copy-start | bytes 196612
  5.6 0.7 %copy-start.4 = (f32[49,128]{1,0:T(8,128)S(1)}, f32[49,128]{1,0:T(8,128)}, u32[]{:S(2)}) copy-start(f32[49,128]{1,0:T(8,128)} %kern.1) | copy-start | bytes 75268

commit v2 on v1

--- a/solution.py
+++ b/solution.py
@@ -12,7 +12,7 @@
 H = KS // 2
 COL = 8
 ROWS_AT_ONCE = 4
-SMALL_ROWS = 56
+SMALL_ROWS = 64
 
 eps = 1e-06
 root_two_pi = 0.7978845608028654
@@ -43,12 +43,13 @@
 
 def body(
     tiles, dps, factor,
-    adj, x_ref, ct_ref, kern, gain_ref, w_in_ref, w_out_ref, scale_ref,
+    adj, x_hbm, ct_hbm, kern, gain_ref, w_in_ref, w_out_ref, scale_ref,
     out_ref, small_out, w_out_all,
     pad, strips, faces, win, wout, conv_ref, part, cg, cpad, gpad, rimf, rims, incoming,
-    chan_recv, dp_send, dp_recv, tile_grads, kacc, small_chan, small_dp, small_tile, base,
+    chan_recv, dp_send, dp_recv, piece_send, piece_recv, piece_all, kacc, small_part, small_recv,
+    small_dp, small_tile, small_done, base, x_ref, ct_ref, local_sem,
     face_send, face_recv, pair_send, pair_recv, rim_send, rim_recv,
-    dp_send_sem, dp_recv_sem, tg_send, tg_recv, sd_send, sd_recv, st_send, st_recv,
+    dp_send_sem, dp_recv_sem, rs_send, rs_recv, tg_send, tg_recv, sd_send, sd_recv, st_send, st_recv,
 ):
     ts = x_ref.shape[0]
     half = ts // 2
@@ -57,6 +58,15 @@
     me_d = lax.axis_index("dp")
     me_c = lax.axis_index("chan")
     sib = 1 - me_c
+
+    x_copy = pltpu.make_async_copy(x_hbm, x_ref, local_sem.at[0])
+    x_copy.start()
+    win_local = pltpu.make_async_copy(w_in_ref, win.at[me_c], local_sem.at[1])
+    win_local.start()
+    wout_local = pltpu.make_async_copy(w_out_ref, wout.at[me_c], local_sem.at[2])
+    wout_local.start()
+    ct_copy = pltpu.make_async_copy(ct_hbm, ct_ref, local_sem.at[3])
+    ct_copy.start()
 
     barrier = pltpu.get_barrier_semaphore()
     for o in range(1, tiles):
@@ -91,6 +101,8 @@
             return carry
         lax.fori_loop(0, count, wrapped, 0)
 
+    x_copy.wait()
+
     def fill(i):
         pad[H + i, COL:COL + ts, :] = x_ref[i].astype(F32)
     rows_loop(ts, fill)
@@ -105,20 +117,24 @@
     rows_loop(ts, face_row)
     for f in range(4):
         faces[me_t, f] = strips[f].astype(BF16)
-    win[me_c] = w_in_ref[...]
-    wout[me_c] = w_out_ref[...]
 
     pl.semaphore_wait(barrier, tiles - 1 + dps - 1 + 1)
-    face_copies = to_peers("tile", tiles, me_t, lambda peer: faces.at[me_t], faces.at[me_t], face_send, face_recv)
-    win_copy = to_sibling(win.at[me_c], win.at[me_c], 0)
-    wout_copy = to_sibling(wout.at[me_c], wout.at[me_c], 1)
+    mine = pl.ds(2 * me_c, 2)
+    face_copies = to_peers("tile", tiles, me_t, lambda peer: faces.at[me_t, mine], faces.at[me_t, mine], face_send, face_recv)
+    win_copy = to_sibling(w_in_ref, win.at[me_c], 0)
+    wout_copy = to_sibling(w_out_ref, wout.at[me_c], 1)
 
     def zero_rows(i):
         cpad[i] = jnp.zeros(cpad.shape[1:], F32)
     rows_loop(cpad.shape[0], zero_rows)
     kacc[...] = jnp.zeros_like(kacc)
 
-    for copy in face_copies:
+    face_passes = []
+    for o in range(1, tiles):
+        face_copies[o - 1].wait_recv()
+        source = lax.rem(me_t - o + tiles, tiles)
+        face_passes.append(to_sibling(faces.at[source, mine], faces.at[source, mine], 5 + o))
+    for copy in face_passes:
         copy.wait_recv()
 
     for k in range(8):
@@ -163,6 +179,9 @@
 
     win_copy.wait_recv()
     wout_copy.wait_recv()
+    win_local.wait()
+    wout_local.wait()
+    ct_copy.wait()
 
     gain = gain_ref[...]
     layer_scale = scale_ref[...]
@@ -219,10 +238,24 @@
         sums = lax.fori_loop(0, half, kernel_row, tuple(jnp.zeros((8, channels), F32) for _ in range(KS)))
         for b in range(KS):
             kacc[a * KS + b] = sums[b]
-    small_chan[0] = jnp.sum(kacc[...], axis=1)
-    small_chan[0, KS * KS:KS * KS + 1, :] = gain_total
-    small_chan[0, KS * KS + 1:KS * KS + 2, :] = scale_total
-    small_copy = to_sibling(small_chan.at[0], small_chan.at[1], 4)
+    for c in range(2):
+        small_part[c] = jnp.sum(kacc[c * SMALL_ROWS // 2:(c + 1) * SMALL_ROWS // 2], axis=1)
+    at = KS * KS - SMALL_ROWS // 2
+    small_part[1, at:at + 1, :] = gain_total
+    small_part[1, at + 1:at + 2, :] = scale_total
+    small_copy = to_sibling(small_part.at[sib], small_recv, 4)
+
+    part_rows = channels // dps
+    part_copy.wait_recv()
+    for w in range(2):
+        for d in range(dps):
+            rows = slice(d * part_rows, (d + 1) * part_rows)
+            dp_send[d, w] = part[me_c, w, rows, :] + chan_recv[w, rows, :]
+    dp_recv[me_d] = dp_send[me_d]
+    dp_copies = to_peers("dp", dps, me_d, lambda peer: dp_send.at[peer], dp_recv.at[me_d], dp_send_sem, dp_recv_sem)
+    small_copy.wait_recv()
+    small_dp[me_d] = small_part[me_c] + small_recv[...]
+    sd_copies = to_peers("dp", dps, me_d, lambda peer: small_dp.at[me_d], small_dp.at[me_d], sd_send, sd_recv)
 
     cg_copy.wait_recv()
 
@@ -243,17 +276,43 @@
                         acc[r] = acc[r] + window * kern[at:at + 1, :]
         for r in range(2):
             gpad[i + r] = acc[r]
-    rows_loop((ts + 2 * H) // 2, spread_rows)
+    spread_blocks = (ts + 2 * H) // 2
+    rows_loop(spread_blocks // 2, spread_rows)
+
+    piece_rows = 2 * part_rows // tiles
+    for copy in dp_copies:
+        copy.wait_recv()
+    total = dp_recv[0]
+    for d in range(1, dps):
+        total = total + dp_recv[d]
+    total = total.reshape(2 * part_rows, total.shape[2]).astype(BF16)
+    for t in range(tiles):
+        piece_send[t] = total[t * piece_rows:(t + 1) * piece_rows]
+    piece_recv[me_t] = piece_send[me_t]
+    rs_copies = to_peers("tile", tiles, me_t, lambda peer: piece_send.at[peer], piece_recv.at[me_t], rs_send, rs_recv)
+    for copy in sd_copies:
+        copy.wait_recv()
+    total = small_dp[0]
+    for d in range(1, dps):
+        total = total + small_dp[d]
+    small_tile[me_t] = total
+    st_copies = to_peers("tile", tiles, me_t, lambda peer: small_tile.at[me_t], small_tile.at[me_t], st_send, st_recv)
+
+    def later_rows(block):
+        spread_rows(block + spread_blocks // 2)
+    rows_loop(spread_blocks - spread_blocks // 2, later_rows)
 
     def edge_row(p):
         for d in range(H):
-            rimf[pl.ds(d * ts + p, 1), :] = gpad[H - 1 - d, pl.ds(H + ts - 1 - p, 1), :]
-            rimf[pl.ds(strip + d * ts + p, 1), :] = gpad[H + ts - 1 - p, H + ts + d:H + ts + d + 1, :]
-            rimf[pl.ds(3 * strip + d * ts + p, 1), :] = gpad[H + p, H - 1 - d:H - d, :]
+            at = d * ts + p
+            rimf[0, pl.ds(at, 1), :] = gpad[H - 1 - d, pl.ds(H + ts - 1 - p, 1), :]
+            rimf[0, pl.ds(strip + at, 1), :] = gpad[H + ts - 1 - p, H + ts + d:H + ts + d + 1, :]
+            rimf[1, pl.ds(strip + at, 1), :] = gpad[H + p, H - 1 - d:H - d, :]
     rows_loop(ts, edge_row)
-    rimf[4 * strip:, :] = jnp.zeros((64, channels), F32)
+    for c in range(2):
+        rimf[c, 2 * strip:, :] = jnp.zeros((32, channels), F32)
     for d in range(H):
-        rimf[2 * strip + d * ts:2 * strip + (d + 1) * ts, :] = gpad[H + ts + d, H:H + ts, :]
+        rimf[1, d * ts:(d + 1) * ts, :] = gpad[H + ts + d, H:H + ts, :]
     for i in range(H):
         for j in range(H):
             spots = (
@@ -261,44 +320,37 @@
                 (H + ts + i, j), (H - 1 - i, H - 1 - j),
             )
             for k in range(4):
-                at = 4 * strip + 16 * k + H * i + j
+                at = 2 * strip + 16 * (k % 2) + H * i + j
                 row, col = spots[k]
-                rimf[at:at + 1, :] = gpad[row, col:col + 1, :]
+                rimf[k // 2, at:at + 1, :] = gpad[row, col:col + 1, :]
     rims[me_t] = rimf[...].astype(BF16)
-    rim_copies = to_peers("tile", tiles, me_t, lambda peer: rims.at[me_t], rims.at[me_t], rim_send, rim_recv)
-
-    part_rows = channels // dps
-    part_copy.wait_recv()
-    for w in range(2):
-        for d in range(dps):
-            rows = slice(d * part_rows, (d + 1) * part_rows)
-            dp_send[d, w] = part[me_c, w, rows, :] + chan_recv[w, rows, :]
-    dp_recv[me_d] = dp_send[me_d]
-    dp_copies = to_peers("dp", dps, me_d, lambda peer: dp_send.at[peer], dp_recv.at[me_d], dp_send_sem, dp_recv_sem)
-    small_copy.wait_recv()
-    small_dp[me_d] = small_chan[0] + small_chan[1]
-    sd_copies = to_peers("dp", dps, me_d, lambda peer: small_dp.at[me_d], small_dp.at[me_d], sd_send, sd_recv)
+    rim_copies = to_peers("tile", tiles, me_t, lambda peer: rims.at[me_t, me_c], rims.at[me_t, me_c], rim_send, rim_recv)
 
     def base_row(i):
         base[i] = ct_ref[i].astype(F32) + gpad[H + i, H:H + ts, :]
     rows_loop(ts, base_row)
 
-    for copy in dp_copies:
-        copy.wait_recv()
-    total = dp_recv[0]
-    for d in range(1, dps):
-        total = total + dp_recv[d]
-    tile_grads[me_t] = total.astype(tile_grads.dtype)
-    tg_copies = to_peers("tile", tiles, me_t, lambda peer: tile_grads.at[me_t], tile_grads.at[me_t], tg_send, tg_recv)
-    for copy in sd_copies:
-        copy.wait_recv()
-    total = small_dp[0]
-    for d in range(1, dps):
-        total = total + small_dp[d]
-    small_tile[me_t] = total
-    st_copies = to_peers("tile", tiles, me_t, lambda peer: small_tile.at[me_t], small_tile.at[me_t], st_send, st_recv)
-
-    for copy in rim_copies:
+    for copy in rs_copies:
+        copy.wait_recv()
+    total = piece_recv[0].astype(F32)
+    for t in range(1, tiles):
+        total = total + piece_recv[t].astype(F32)
+    piece_all[me_t] = (total * factor).astype(BF16)
+    tg_copies = to_peers("tile", tiles, me_t, lambda peer: piece_all.at[me_t], piece_all.at[me_t], tg_send, tg_recv)
+    for copy in st_copies:
+        copy.wait_recv()
+    total = small_tile[0]
+    for t in range(1, tiles):
+        total = total + small_tile[t]
+    small_done[me_c] = total * factor
+    done_copy = to_sibling(small_done.at[me_c], small_done.at[me_c], 5)
+
+    rim_passes = []
+    for o in range(1, tiles):
+        rim_copies[o - 1].wait_recv()
+        source = lax.rem(me_t - o + tiles, tiles)
+        rim_passes.append(to_sibling(rims.at[source, me_c], rims.at[source, me_c], 5 + tiles - 1 + o))
+    for copy in rim_passes:
         copy.wait_recv()
     for f in range(4):
         def gather(p, carry):
@@ -307,10 +359,10 @@
                 face = (adj[p, k, 1] + facing_turns[k]) % 4
                 chosen = jnp.where((adj[p, k, 0] == me_t) & (face == f), 1.0, 0.0).astype(F32)
                 if k < 4:
-                    edge = edge + chosen * rims[p, strip * k:strip * (k + 1), :].astype(F32)
+                    edge = edge + chosen * rims[p, k // 2, strip * (k % 2):strip * (k % 2 + 1), :].astype(F32)
                 else:
-                    at = 4 * strip + 16 * (k - 4)
-                    piece = chosen * rims[p, at:at + 16, :].astype(F32)
+                    at = 2 * strip + 16 * (k % 2)
+                    piece = chosen * rims[p, (k - 4) // 2, at:at + 16, :].astype(F32)
                     if corner_at_end[k - 4]:
                         at_end = at_end + piece
                     else:
@@ -338,19 +390,13 @@
 
     for copy in tg_copies:
         copy.wait_recv()
-    total = tile_grads[0].astype(F32)
-    for t in range(1, tiles):
-        total = total + tile_grads[t].astype(F32)
-    w_out_all[...] = total * factor
-    for copy in st_copies:
-        copy.wait_recv()
-    total = small_tile[0]
-    for t in range(1, tiles):
-        total = total + small_tile[t]
-    small_out[...] = total * factor
-
-    for copy in face_copies + rim_copies + dp_copies + sd_copies + tg_copies + st_copies + [
-        win_copy, wout_copy, cg_copy, part_copy, small_copy
+    for t in range(tiles):
+        w_out_all[t * piece_rows:(t + 1) * piece_rows, :] = piece_all[t].astype(F32)
+    done_copy.wait_recv()
+    small_out[...] = small_done[...]
+
+    for copy in face_copies + face_passes + rim_copies + rim_passes + rs_copies + dp_copies + sd_copies + tg_copies + st_copies + [
+        win_copy, wout_copy, cg_copy, part_copy, small_copy, done_copy
     ]:
         copy.wait_send()
 
@@ -361,19 +407,22 @@
     tiles, dps = lax.axis_size("tile"), lax.axis_size("dp")
     factor = 1.0 / math.sqrt(dps * tiles * ts * ts)
     strip = H * ts
-    rim_rows = 4 * strip + 64
+    rim_rows = 2 * strip + 32
+    piece = 2 * (ch // dps) // tiles
+    half_small = SMALL_ROWS // 2
     part_rows = ch // dps
     vmem = pl.BlockSpec(memory_space=pltpu.VMEM)
+    hbm = pl.BlockSpec(memory_space=pltpu.MemorySpace.HBM)
     dma = pltpu.SemaphoreType.DMA
     peers_t, peers_d = max(tiles - 1, 1), max(dps - 1, 1)
     out, small, grads = pl.pallas_call(
         functools.partial(body, tiles, dps, factor),
         out_shape=(
             jax.ShapeDtypeStruct((ts, ts, ch), BF16),
-            jax.ShapeDtypeStruct((SMALL_ROWS, ch), F32),
-            jax.ShapeDtypeStruct((2, part_rows, hid), F32),
+            jax.ShapeDtypeStruct((2, SMALL_ROWS // 2, ch), F32),
+            jax.ShapeDtypeStruct((2 * part_rows, hid), F32),
         ),
-        in_specs=[pl.BlockSpec(memory_space=pltpu.SMEM)] + [vmem] * 7,
+        in_specs=[pl.BlockSpec(memory_space=pltpu.SMEM), hbm, hbm, vmem, vmem, hbm, hbm, vmem],
         out_specs=(vmem,) * 3,
         scratch_shapes=[
             pltpu.VMEM((ts + 2 * H, ts + 2 * COL, ch), F32),
@@ -386,35 +435,43 @@
             pltpu.VMEM((ts, ts, ch), BF16),
             pltpu.VMEM((ts + 2 * (KS - 1), ts + 2 * COL, ch), F32),
             pltpu.VMEM((ts + 2 * H, ts + 8, ch), F32),
-            pltpu.VMEM((rim_rows, ch), F32),
-            pltpu.VMEM((tiles, rim_rows, ch), BF16),
+            pltpu.VMEM((2, rim_rows, ch), F32),
+            pltpu.VMEM((tiles, 2, rim_rows, ch), BF16),
             pltpu.VMEM((4, strip, ch), F32),
             pltpu.VMEM((2, ch, hid), F32),
             pltpu.VMEM((dps, 2, part_rows, hid), F32),
             pltpu.VMEM((dps, 2, part_rows, hid), F32),
-            pltpu.VMEM((tiles, 2, part_rows, hid), BF16),
+            pltpu.VMEM((tiles, piece, hid), BF16),
+            pltpu.VMEM((tiles, piece, hid), BF16),
+            pltpu.VMEM((tiles, piece, hid), BF16),
             pltpu.VMEM((SMALL_ROWS, 8, ch), F32),
-            pltpu.VMEM((2, SMALL_ROWS, ch), F32),
-            pltpu.VMEM((dps, SMALL_ROWS, ch), F32),
-            pltpu.VMEM((tiles, SMALL_ROWS, ch), F32),
+            pltpu.VMEM((2, half_small, ch), F32),
+            pltpu.VMEM((half_small, ch), F32),
+            pltpu.VMEM((dps, half_small, ch), F32),
+            pltpu.VMEM((tiles, half_small, ch), F32),
+            pltpu.VMEM((2, half_small, ch), F32),
             pltpu.VMEM((ts, ts, ch), F32),
-            dma((peers_t,)), dma((peers_t,)), dma((5,)), dma((5,)), dma((peers_t,)), dma((peers_t,)),
-            dma((peers_d,)), dma((peers_d,)), dma((peers_t,)), dma((peers_t,)),
+            pltpu.VMEM((ts, ts, ch), BF16),
+            pltpu.VMEM((ts, ts, ch), BF16),
+            dma((4,)),
+            dma((peers_t,)), dma((peers_t,)), dma((4 + 2 * tiles,)), dma((4 + 2 * tiles,)), dma((peers_t,)), dma((peers_t,)),
+            dma((peers_d,)), dma((peers_d,)), dma((peers_t,)), dma((peers_t,)), dma((peers_t,)), dma((peers_t,)),
             dma((peers_d,)), dma((peers_d,)), dma((peers_t,)), dma((peers_t,)),
         ],
         compiler_params=pltpu.CompilerParams(
-            collective_id=0, has_side_effects=True, vmem_limit_bytes=48 * 1024 * 1024
+            collective_id=0, has_side_effects=True, vmem_limit_bytes=64 * 1024 * 1024 - 64 * 1024
         ),
     )(
         adjacency, inputs[0, 0], cotangent[0, 0], kernel, norm_gain[None], w_in, w_out, layer_scale[None]
     )
     taps = KS * KS
+    small = small.reshape(SMALL_ROWS, ch)
     return (
         out[None, None],
         small[:taps],
         small[taps],
-        grads[0],
-        grads[1].T,
+        grads[:part_rows],
+        grads[part_rows:].T,
         small[taps + 1],
     )
 

time: 51.6 us -> 42.9 us (0.83)
  the two profiles are of different devices: /device:TPU:0 before, /device:TPU:1 now
where the time goes in v2:
time: 42.9 us; the launch traced here: 42.5 us
  Pallas kernels  35.6 us (83%)
  local copies, waits for them, and re-layouts  6.25 us (15%)
  between operations  0.65 us (2%)
    pallas_call x1, Pallas kernels, on_device(): pl.pallas_call(functools.partial(body, tiles, dps, factor), out_shape=(ja...  35.6 us
    unnamed x4, local copies, waits for them, and re-layouts  2.09 us
    transpose x1, local copies, waits for them, and re-layouts, on_device(): grads[part_rows:]  1.53 us
    slice x1, local copies, waits for them, and re-layouts, on_device(): small[:taps]  1.36 us
    squeeze x1, local copies, waits for them, and re-layouts, on_device(): small[taps + 1]  1.28 us

profile of v2, /device:TPU:1, one launch (start us, length us, event | category | flops | bytes accessed | tf_op | source)
XLA Modules:
  0.0 42.5 jit_solution(600256074535014434)
XLA Ops:
  0.6 1.4 %copy.14.adj = s32[4,8,2]{2,1,0:T(8,128)} copy(s32[4,8,2]{1,2,0:T(2,128)} %param.15) | data formatting | bytes 512 | tf_op args[7]
  2.0 35.6 %shard_map.127 = (bf16[32,32,128]{2,1,0:T(8,128)(2,1)}, f32[2,32,128]{2,1,0:T(8,128)}, f32[128,256]{1,0:T(8,128)}) custom-call(s32[4,8,2]{2,1,0:T(8,128)} %copy.14.adj, bf16[32,32,128]{2,1,0:T(8,128)(2,1)} %bitcast.12, bf16[32,32,128]{2,1,0:T(8,128)(2,1)} %bitcast.13, f32[49,128]{1,0:T(8,128)} %kern.1, f32[1,128]{1,0:T(1,128)} %bitcast.17, ...), custom_call_target="tpu_custom_call" | custom-call | tf_op jit(solution)/shard_map/pallas_call | solution.py:418
  37.6 0.0 copy-start
  37.6 1.3 %slice_bitcast_fusion.1 = (f32[128]{0:T(128)}, f32[128]{0:T(128)}) fusion(f32[64,128]{1,0:T(8,128)} %bitcast.15), kind=kLoop, calls=%fused_computation.1 | loop fusion | bytes 2048 | tf_op jit(solution)/shard_map/squeeze | solution.py:475
  38.9 1.5 %slice_bitcast_fusion = (f32[256,64]{0,1:T(8,128)}, f32[64,256]{1,0:T(8,128)}) fusion(f32[128,256]{1,0:T(8,128)} %get-tuple-element.11), kind=kLoop, calls=%fused_computation | loop fusion | bytes 262144 | tf_op jit(solution)/shard_map/transpose | solution.py:474
  40.4 1.4 %slice.20 = f32[49,128]{1,0:T(8,128)} slice(f32[64,128]{1,0:T(8,128)} %bitcast.16), slice={[0:49], [0:128]} | slice | bytes 50176 | tf_op jit(solution)/shard_map/slice | solution.py:471
  41.8 0.0 copy-done
  41.8 0.7 %copy.16 = bf16[1,1,32,32,128]{4,3,2,1,0:T(8,128)(2,1)} copy(bf16[1,1,32,32,128]{4,3,2,1,0:T(8,128)(2,1)S(1)} %bitcast.14) | data formatting | bytes 524288
Async XLA Ops:
  37.6 4.2 %copy-start = (bf16[32,32,128]{2,1,0:T(8,128)(2,1)S(1)}, bf16[32,32,128]{2,1,0:T(8,128)(2,1)}, u32[]{:S(2)}) copy-start(bf16[32,32,128]{2,1,0:T(8,128)(2,1)} %get-tuple-element.9) | copy-start | bytes 786436

commit v3 on v2

--- a/solution.py
+++ b/solution.py
@@ -138,8 +138,8 @@
         copy.wait_recv()
 
     for k in range(8):
-        source = adj[me_t, k, 0]
-        face = (adj[me_t, k, 1] + facing_turns[k]) % 4
+        source = adj[me_t, 0, k]
+        face = (adj[me_t, 1, k] + facing_turns[k]) % 4
         strips[k] = faces[source, face].astype(F32)
     for d in range(H):
         pad[H + ts + d, COL:COL + ts, :] = strips[2, d * ts:(d + 1) * ts, :]
@@ -245,18 +245,6 @@
     small_part[1, at + 1:at + 2, :] = scale_total
     small_copy = to_sibling(small_part.at[sib], small_recv, 4)
 
-    part_rows = channels // dps
-    part_copy.wait_recv()
-    for w in range(2):
-        for d in range(dps):
-            rows = slice(d * part_rows, (d + 1) * part_rows)
-            dp_send[d, w] = part[me_c, w, rows, :] + chan_recv[w, rows, :]
-    dp_recv[me_d] = dp_send[me_d]
-    dp_copies = to_peers("dp", dps, me_d, lambda peer: dp_send.at[peer], dp_recv.at[me_d], dp_send_sem, dp_recv_sem)
-    small_copy.wait_recv()
-    small_dp[me_d] = small_part[me_c] + small_recv[...]
-    sd_copies = to_peers("dp", dps, me_d, lambda peer: small_dp.at[me_d], small_dp.at[me_d], sd_send, sd_recv)
-
     cg_copy.wait_recv()
 
     def widen(i):
@@ -279,24 +267,17 @@
     spread_blocks = (ts + 2 * H) // 2
     rows_loop(spread_blocks // 2, spread_rows)
 
-    piece_rows = 2 * part_rows // tiles
-    for copy in dp_copies:
-        copy.wait_recv()
-    total = dp_recv[0]
-    for d in range(1, dps):
-        total = total + dp_recv[d]
-    total = total.reshape(2 * part_rows, total.shape[2]).astype(BF16)
-    for t in range(tiles):
-        piece_send[t] = total[t * piece_rows:(t + 1) * piece_rows]
-    piece_recv[me_t] = piece_send[me_t]
-    rs_copies = to_peers("tile", tiles, me_t, lambda peer: piece_send.at[peer], piece_recv.at[me_t], rs_send, rs_recv)
-    for copy in sd_copies:
-        copy.wait_recv()
-    total = small_dp[0]
-    for d in range(1, dps):
-        total = total + small_dp[d]
-    small_tile[me_t] = total
-    st_copies = to_peers("tile", tiles, me_t, lambda peer: small_tile.at[me_t], small_tile.at[me_t], st_send, st_recv)
+    part_rows = channels // dps
+    part_copy.wait_recv()
+    for w in range(2):
+        for d in range(dps):
+            rows = slice(d * part_rows, (d + 1) * part_rows)
+            dp_send[d, w] = part[me_c, w, rows, :] + chan_recv[w, rows, :]
+    dp_recv[me_d] = dp_send[me_d]
+    dp_copies = to_peers("dp", dps, me_d, lambda peer: dp_send.at[peer], dp_recv.at[me_d], dp_send_sem, dp_recv_sem)
+    small_copy.wait_recv()
+    small_dp[me_d] = small_part[me_c] + small_recv[...]
+    sd_copies = to_peers("dp", dps, me_d, lambda peer: small_dp.at[me_d], small_dp.at[me_d], sd_send, sd_recv)
 
     def later_rows(block):
         spread_rows(block + spread_blocks // 2)
@@ -326,6 +307,25 @@
     rims[me_t] = rimf[...].astype(BF16)
     rim_copies = to_peers("tile", tiles, me_t, lambda peer: rims.at[me_t, me_c], rims.at[me_t, me_c], rim_send, rim_recv)
 
+    piece_rows = 2 * part_rows // tiles
+    for copy in dp_copies:
+        copy.wait_recv()
+    total = dp_recv[0]
+    for d in range(1, dps):
+        total = total + dp_recv[d]
+    total = total.reshape(2 * part_rows, total.shape[2]).astype(BF16)
+    for t in range(tiles):
+        piece_send[t] = total[t * piece_rows:(t + 1) * piece_rows]
+    piece_recv[me_t] = piece_send[me_t]
+    rs_copies = to_peers("tile", tiles, me_t, lambda peer: piece_send.at[peer], piece_recv.at[me_t], rs_send, rs_recv)
+    for copy in sd_copies:
+        copy.wait_recv()
+    total = small_dp[0]
+    for d in range(1, dps):
+        total = total + small_dp[d]
+    small_tile[me_t] = total
+    st_copies = to_peers("tile", tiles, me_t, lambda peer: small_tile.at[me_t], small_tile.at[me_t], st_send, st_recv)
+
     def base_row(i):
         base[i] = ct_ref[i].astype(F32) + gpad[H + i, H:H + ts, :]
     rows_loop(ts, base_row)
@@ -356,8 +356,8 @@
         def gather(p, carry):
             edge, at_start, at_end = carry
             for k in range(8):
-                face = (adj[p, k, 1] + facing_turns[k]) % 4
-                chosen = jnp.where((adj[p, k, 0] == me_t) & (face == f), 1.0, 0.0).astype(F32)
+                face = (adj[p, 1, k] + facing_turns[k]) % 4
+                chosen = jnp.where((adj[p, 0, k] == me_t) & (face == f), 1.0, 0.0).astype(F32)
                 if k < 4:
                     edge = edge + chosen * rims[p, k // 2, strip * (k % 2):strip * (k % 2 + 1), :].astype(F32)
                 else:
@@ -399,6 +399,10 @@
         win_copy, wout_copy, cg_copy, part_copy, small_copy, done_copy
     ]:
         copy.wait_send()
+
+
+def in_hbm(array):
+    return pltpu.with_memory_space_constraint(array, pltpu.MemorySpace.HBM)
 
 
 def on_device(inputs, kernel, norm_gain, w_in, w_out, layer_scale, cotangent, adjacency):
@@ -459,10 +463,11 @@
             dma((peers_d,)), dma((peers_d,)), dma((peers_t,)), dma((peers_t,)),
         ],
         compiler_params=pltpu.CompilerParams(
-            collective_id=0, has_side_effects=True, vmem_limit_bytes=64 * 1024 * 1024 - 64 * 1024
+            collective_id=0, has_side_effects=True, vmem_limit_bytes=48 * 1024 * 1024
         ),
     )(
-        adjacency, inputs[0, 0], cotangent[0, 0], kernel, norm_gain[None], w_in, w_out, layer_scale[None]
+        jnp.transpose(adjacency, (0, 2, 1)), in_hbm(inputs[0, 0]), in_hbm(cotangent[0, 0]), kernel,
+        norm_gain[None], in_hbm(w_in), in_hbm(w_out), layer_scale[None],
     )
     taps = KS * KS
     small = small.reshape(SMALL_ROWS, ch)

time: 42.9 us -> 38.6 us (0.90)
  the two profiles are of different devices: /device:TPU:1 before, /device:TPU:0 now
where the time goes in v3:
time: 38.6 us; the launch traced here: 38.4 us
  Pallas kernels  33.8 us (88%)
  local copies, waits for them, and re-layouts  3.91 us (10%)
  between operations  0.67 us (2%)
    pallas_call x1, Pallas kernels, on_device(): pl.pallas_call(functools.partial(body, tiles, dps, factor), out_shape=(ja...  33.8 us
    unnamed x9, local copies, waits for them, and re-layouts  2.12 us

profile of v3, /device:TPU:0, one launch (start us, length us, event | category | flops | bytes accessed | tf_op | source)
XLA Modules:
  0.0 38.4 jit_solution(16118368438933420374)
XLA Ops:
  0.6 0.0 copy-start.1
  0.6 0.0 copy-start.2
  0.7 0.0 copy-start.3
  0.7 0.7 %copy-done.1 = s32[4,8,2]{1,2,0:T(2,128)S(1)} copy-done((s32[4,8,2]{1,2,0:T(2,128)S(1)}, s32[4,8,2]{1,2,0:T(2,128)}, u32[]{:S(2)}) %copy-start.1) | copy-done | bytes 280
  1.3 0.0 copy-done.2
  1.3 0.0 copy-done.3
  1.3 0.0 copy-start
  1.3 0.7 %copy-done = f32[49,128]{1,0:T(8,128)S(1)} copy-done((f32[49,128]{1,0:T(8,128)S(1)}, f32[49,128]{1,0:T(8,128)}, u32[]{:S(2)}) %copy-start) | copy-done | bytes 25112
  2.1 33.8 %shard_map.127 = (bf16[32,32,128]{2,1,0:T(8,128)(2,1)S(1)}, f32[2,32,128]{2,1,0:T(8,128)S(1)}, f32[128,256]{1,0:T(8,128)S(1)}) custom-call(s32[4,2,8]{2,1,0:T(2,128)S(1)} %bitcast.16, bf16[32,32,128]{2,1,0:T(8,128)(2,1)} %bitcast.19, bf16[32,32,128]{2,1,0:T(8,128)(2,1)} %bitcast.20, f32[49,128]{1,0:T(8,128)S(1)} %copy-done, f32[1,128]{1,0:T(1,128)S(1)} %bitcast.17, ...), custom_call_target="tpu_custom_call" | custom-call | tf_op jit(solution)/shard_map/pallas_call | solution.py:422
  35.9 0.5 %slice_bitcast_fusion.1 = (f32[128]{0:T(128)}, f32[128]{0:T(128)}) fusion(f32[64,128]{1,0:T(8,128)S(1)} %bitcast.14), kind=kLoop, calls=%fused_computation.1 | loop fusion | bytes 2048 | tf_op jit(solution)/shard_map/squeeze | solution.py:480
  36.4 0.7 %slice_bitcast_fusion = (f32[256,64]{0,1:T(8,128)}, f32[64,256]{1,0:T(8,128)}) fusion(f32[128,256]{1,0:T(8,128)S(1)} %get-tuple-element.11), kind=kLoop, calls=%fused_computation | loop fusion | bytes 262144 | tf_op jit(solution)/shard_map/transpose | solution.py:479
  37.1 0.6 %slice.20 = f32[49,128]{1,0:T(8,128)} slice(f32[64,128]{1,0:T(8,128)S(1)} %bitcast.15), slice={[0:49], [0:128]} | slice | bytes 50176 | tf_op jit(solution)/shard_map/slice | solution.py:476
  37.7 0.7 %copy.15 = bf16[1,1,32,32,128]{4,3,2,1,0:T(8,128)(2,1)} copy(bf16[1,1,32,32,128]{4,3,2,1,0:T(8,128)(2,1)S(1)} %bitcast.13) | data formatting | bytes 524288
Async XLA Ops:
  0.6 0.7 %copy-start.1 = (s32[4,8,2]{1,2,0:T(2,128)S(1)}, s32[4,8,2]{1,2,0:T(2,128)}, u32[]{:S(2)}) copy-start(s32[4,8,2]{1,2,0:T(2,128)} %param.15) | copy-start | bytes 772
  0.6 0.7 %copy-start.2 = (f32[128]{0:T(128)S(1)}, f32[128]{0:T(128)}, u32[]{:S(2)}) copy-start(f32[128]{0:T(128)} %param.10) | copy-start | bytes 1540
  0.7 0.7 %copy-start.3 = (f32[128]{0:T(128)S(1)}, f32[128]{0:T(128)}, u32[]{:S(2)}) copy-start(f32[128]{0:T(128)} %param.13) | copy-start | bytes 1540
  1.3 0.7 %copy-start = (f32[49,128]{1,0:T(8,128)S(1)}, f32[49,128]{1,0:T(8,128)}, u32[]{:S(2)}) copy-start(f32[49,128]{1,0:T(8,128)} %kern.1) | copy-start | bytes 75268

commit v4 on v3

--- a/solution.py
+++ b/solution.py
@@ -253,18 +253,18 @@
     wide = gpad.shape[1]
 
     def spread_rows(block):
-        i = block * 2
-        acc = [jnp.zeros((wide, channels), F32) for _ in range(2)]
-        for a in range(KS + 1):
+        i = block * ROWS_AT_ONCE
+        acc = [jnp.zeros((wide, channels), F32) for _ in range(ROWS_AT_ONCE)]
+        for a in range(ROWS_AT_ONCE + KS - 1):
             for b in range(KS):
                 window = cpad[i + a, COL - (KS - 1) + b:COL - (KS - 1) + b + wide, :]
-                for r in range(2):
+                for r in range(ROWS_AT_ONCE):
                     if 0 <= a - r < KS:
                         at = (KS - 1 - (a - r)) * KS + KS - 1 - b
                         acc[r] = acc[r] + window * kern[at:at + 1, :]
-        for r in range(2):
+        for r in range(ROWS_AT_ONCE):
             gpad[i + r] = acc[r]
-    spread_blocks = (ts + 2 * H) // 2
+    spread_blocks = gpad.shape[0] // ROWS_AT_ONCE
     rows_loop(spread_blocks // 2, spread_rows)
 
     part_rows = channels // dps
@@ -437,8 +437,8 @@
             pltpu.VMEM((ts // 2, ts, ch), F32),
             pltpu.VMEM((2, 2, ch, hid), F32),
             pltpu.VMEM((ts, ts, ch), BF16),
-            pltpu.VMEM((ts + 2 * (KS - 1), ts + 2 * COL, ch), F32),
-            pltpu.VMEM((ts + 2 * H, ts + 8, ch), F32),
+            pltpu.VMEM((ts + 2 * (KS - 1) + 2, ts + 2 * COL, ch), F32),
+            pltpu.VMEM((ts + 2 * H + 2, ts + 8, ch), F32),
             pltpu.VMEM((2, rim_rows, ch), F32),
             pltpu.VMEM((tiles, 2, rim_rows, ch), BF16),
             pltpu.VMEM((4, strip, ch), F32),

time: 38.6 us -> 38.2 us (0.990)
  Pallas kernels: 33.8 us -> 33.4 us
    pallas_call x1, Pallas kernels: 33.8 us -> 33.4 us  [on_device(): pl.pallas_call(functools.partial(body, tiles, dps, factor), out_shape=(ja...]
where the time goes in v4:
time: 38.2 us; the launch traced here: 37.9 us
  Pallas kernels  33.4 us (87%)
  local copies, waits for them, and re-layouts  3.91 us (10%)
  between operations  0.67 us (2%)
    pallas_call x1, Pallas kernels, on_device(): pl.pallas_call(functools.partial(body, tiles, dps, factor), out_shape=(ja...  33.4 us
    unnamed x9, local copies, waits for them, and re-layouts  2.12 us

profile of v4, /device:TPU:0, one launch (start us, length us, event | category | flops | bytes accessed | tf_op | source)
XLA Modules:
  0.0 37.9 jit_solution(9154246868918306069)
XLA Ops:
  0.6 0.0 copy-start.1
  0.6 0.0 copy-start.2
  0.7 0.0 copy-start.3
  0.7 0.7 %copy-done.1 = s32[4,8,2]{1,2,0:T(2,128)S(1)} copy-done((s32[4,8,2]{1,2,0:T(2,128)S(1)}, s32[4,8,2]{1,2,0:T(2,128)}, u32[]{:S(2)}) %copy-start.1) | copy-done | bytes 280
  1.3 0.0 copy-done.2
  1.3 0.0 copy-done.3
  1.3 0.0 copy-start
  1.3 0.7 %copy-done = f32[49,128]{1,0:T(8,128)S(1)} copy-done((f32[49,128]{1,0:T(8,128)S(1)}, f32[49,128]{1,0:T(8,128)}, u32[]{:S(2)}) %copy-start) | copy-done | bytes 25112
  2.1 33.4 %shard_map.127 = (bf16[32,32,128]{2,1,0:T(8,128)(2,1)S(1)}, f32[2,32,128]{2,1,0:T(8,128)S(1)}, f32[128,256]{1,0:T(8,128)S(1)}) custom-call(s32[4,2,8]{2,1,0:T(2,128)S(1)} %bitcast.16, bf16[32,32,128]{2,1,0:T(8,128)(2,1)} %bitcast.19, bf16[32,32,128]{2,1,0:T(8,128)(2,1)} %bitcast.20, f32[49,128]{1,0:T(8,128)S(1)} %copy-done, f32[1,128]{1,0:T(1,128)S(1)} %bitcast.17, ...), custom_call_target="tpu_custom_call" | custom-call | tf_op jit(solution)/shard_map/pallas_call | solution.py:422
  35.4 0.5 %slice_bitcast_fusion.1 = (f32[128]{0:T(128)}, f32[128]{0:T(128)}) fusion(f32[64,128]{1,0:T(8,128)S(1)} %bitcast.14), kind=kLoop, calls=%fused_computation.1 | loop fusion | bytes 2048 | tf_op jit(solution)/shard_map/squeeze | solution.py:480
  36.0 0.7 %slice_bitcast_fusion = (f32[256,64]{0,1:T(8,128)}, f32[64,256]{1,0:T(8,128)}) fusion(f32[128,256]{1,0:T(8,128)S(1)} %get-tuple-element.11), kind=kLoop, calls=%fused_computation | loop fusion | bytes 262144 | tf_op jit(solution)/shard_map/transpose | solution.py:479
  36.6 0.6 %slice.20 = f32[49,128]{1,0:T(8,128)} slice(f32[64,128]{1,0:T(8,128)S(1)} %bitcast.15), slice={[0:49], [0:128]} | slice | bytes 50176 | tf_op jit(solution)/shard_map/slice | solution.py:476
  37.2 0.7 %copy.15 = bf16[1,1,32,32,128]{4,3,2,1,0:T(8,128)(2,1)} copy(bf16[1,1,32,32,128]{4,3,2,1,0:T(8,128)(2,1)S(1)} %bitcast.13) | data formatting | bytes 524288
Async XLA Ops:
  0.6 0.7 %copy-start.1 = (s32[4,8,2]{1,2,0:T(2,128)S(1)}, s32[4,8,2]{1,2,0:T(2,128)}, u32[]{:S(2)}) copy-start(s32[4,8,2]{1,2,0:T(2,128)} %param.15) | copy-start | bytes 772
  0.6 0.7 %copy-start.2 = (f32[128]{0:T(128)S(1)}, f32[128]{0:T(128)}, u32[]{:S(2)}) copy-start(f32[128]{0:T(128)} %param.10) | copy-start | bytes 1540
  0.7 0.7 %copy-start.3 = (f32[128]{0:T(128)S(1)}, f32[128]{0:T(128)}, u32[]{:S(2)}) copy-start(f32[128]{0:T(128)} %param.13) | copy-start | bytes 1540
  1.3 0.7 %copy-start = (f32[49,128]{1,0:T(8,128)S(1)}, f32[49,128]{1,0:T(8,128)}, u32[]{:S(2)}) copy-start(f32[49,128]{1,0:T(8,128)} %kern.1) | copy-start | bytes 75268
